TPU v7x, 32 devices: a whole 2x2x4 slice. The times are simulated.
32 devices in a mesh: seq: 16 (over z, y, x), grp: 2 (over core).
Axes of the slice: x: 2, y: 2, z: 4, core: 2. Of those that a mesh axis runs over, the one named last changes fastest.
Arguments:
- key_rows: bfloat16 [32768, 4096], P('seq', 'grp')
- probe_ints: int32 [4096, 512], P('grp'), may hold values from -2 to 2
- rank_keep: int32 [1], replicated, may hold values from 128 to 511
Outputs:
- latents: float32 [32768, 512], P('seq', 'grp')
- latent_basis: float32 [512, 4096], P('seq', 'grp')
All inputs are finite; a program needn't handle non-finite values.
Results may differ from a plain program's by a relative error of at most 0.00098.
Values may be sent and summed in bfloat16 or wider, within the bound.
A program may use at most 128 MiB of HBM per device.

v0:
```python
import math

import jax
import jax.numpy as jnp
from jax import lax
from jax.sharding import PartitionSpec as P


def on_device(key_rows, probe_ints, rank_keep):
    seq_count = lax.axis_size("seq")
    tokens = key_rows.shape[0] * seq_count
    root_tokens = math.sqrt(tokens)
    probes = (probe_ints.astype(jnp.float32) * 0.015625).astype(jnp.bfloat16)
    whole_keys = lax.all_gather(key_rows, "grp", axis=1, tiled=True)
    whole_probes = lax.all_gather(probes, "grp", axis=0, tiled=True)
    sketch = jnp.dot(whole_keys, whole_probes, preferred_element_type=jnp.float32)
    contract = (((0,), (0,)), ((), ()))
    local_gram = lax.dot_general(sketch, sketch, contract, precision=lax.Precision.HIGHEST)
    gram_matrix = lax.psum(local_gram, "seq")
    lower_factor = jnp.linalg.cholesky(gram_matrix)
    identity = jnp.eye(gram_matrix.shape[0], dtype=jnp.float32)
    inverse = lax.linalg.triangular_solve(lower_factor, identity, left_side=True, lower=True)
    orthonormal = jnp.dot(sketch, inverse.T, precision=lax.Precision.HIGHEST) * root_tokens
    probe_count = orthonormal.shape[1]
    part_width = probe_count // lax.axis_size("grp")
    first_column = lax.axis_index("grp") * part_width
    columns = first_column + jnp.arange(part_width)
    own_columns = lax.dynamic_slice_in_dim(orthonormal, first_column, part_width, 1)
    latents = jnp.where(columns[None, :] < rank_keep[0], own_columns, jnp.float32(0.0))
    rounded = orthonormal.astype(jnp.bfloat16)
    rows_out = probe_count // seq_count
    summed = lax.psum_scatter(
        lax.dot_general(rounded, key_rows, contract, preferred_element_type=jnp.float32),
        "seq",
        scatter_dimension=0,
        tiled=True,
    )
    row_index = lax.axis_index("seq") * rows_out + jnp.arange(rows_out)
    latent_basis = jnp.where(
        row_index[:, None] < rank_keep[0], summed / root_tokens, jnp.float32(0.0)
    )
    return (latents, latent_basis)


def solution(mesh):
    in_specs = (P("seq", "grp"), P("grp", None), P())
    out_specs = (P("seq", "grp"), P("seq", "grp"))
    return jax.shard_map(
        on_device, mesh=mesh, in_specs=in_specs, out_specs=out_specs, check_vma=False
    )
```

profile of v0, /device:TPU:0, one launch (start us, length us, event | category | flops | bytes accessed | tf_op | source)
XLA Modules:
  0.0 463.2 jit_solution(5321967595677841850)
XLA Ops:
  7.2 0.0 all-gather.3.cloned.1.call-start
  7.2 4.1 multiply_convert_fusion
  11.3 0.0 all-gather.3.cloned.1.call-update
  11.3 0.0 all-gather.5.cloned.1.call-start
  11.4 0.7 all-gather.5.cloned.1.call-update
  12.1 0.0 all-reduce.3.cloned.1.call-start
  12.1 15.7 %all-gather.3.cloned.1.call-done = bf16[4096,512]{1,0:T(8,128)(2,1)} async-done(((bf16[2048,512]{1,0:T(8,128)(2,1)}), bf16[4096,512]{1,0:T(8,128)(2,1)}) %all-gather.3.cloned.1.call-update) | async-done | bytes 4194320 | tf_op jit(solution)/shard_map/all_gather | solution.py:15
  27.8 32.8 %all-gather.5.cloned.1.call-done = bf16[2048,4096]{1,0:T(8,128)(2,1)} async-done(((bf16[2048,2048]{1,0:T(8,128)(2,1)}), bf16[2048,4096]{1,0:T(8,128)(2,1)}) %all-gather.5.cloned.1.call-update) | async-done | bytes 16777232 | tf_op jit(solution)/shard_map/all_gather | solution.py:14
  60.7 13.0 %fusion.42 = f32[512,2048]{1,0:T(8,128)S(1)} fusion(bf16[4096,512]{1,0:T(8,128)(2,1)} %all-gather.3.cloned.1.call-done, bf16[2048,4096]{1,0:T(8,128)(2,1)} %all-gather.5.cloned.1.call-done), kind=kOutput, calls=%fused_computation.84 | convolution fusion | flops 8589934592 | bytes 25165824 | tf_op jit(solution)/shard_map/dot_general | solution.py:16
  73.7 1.9 copy-done
  75.7 7.7 %fusion.43 = f32[512,512]{0,1:T(8,128)} fusion(f32[512,2048]{1,0:T(8,128)S(1)} %fusion.42), kind=kOutput, calls=%fused_computation.85 | convolution fusion | flops 6442450944 | bytes 5242880 | tf_op jit(solution)/shard_map/dot_general | solution.py:18
  83.4 0.0 all-reduce.3.cloned.1.call-update
  83.4 0.2 reduce-scatter.2.cloned.1.call-start
  83.6 0.8 iota_compare_fusion
  84.4 0.1 fusion.18
  84.5 111.9 %all-reduce.3.cloned.1.call-done = f32[512,512]{0,1:T(8,128)} async-done(((f32[512,512]{0,1:T(8,128)}), f32[512,512]{0,1:T(8,128)}) %all-reduce.3.cloned.1.call-update) | async-done | bytes 1048592 | tf_op jit(solution)/shard_map/psum | solution.py:19
  196.4 1.6 copy.6
  198.0 1.4 fusion.9
  199.5 11.7 %cholesky.104 = f32[128,128]{1,0:T(8,128)S(1)} custom-call(f32[128,128]{1,0:T(8,128)S(1)} %cholesky.266), custom_call_target="Cholesky" | custom-call | tf_op jit(solution)/shard_map/jit(cholesky)/cholesky | solution.py:20
  211.2 9.8 %custom-call.30 = f32[1,128,128]{1,2,0:T(8,128)S(1)} custom-call(f32[1,128,128]{2,1,0:T(8,128)S(1)} %get-tuple-element.29), custom_call_target="InvertDiagBlocksLowerTriangular" | custom-call | tf_op jit(solution)/shard_map/jit(cholesky)/cholesky | solution.py:20
  221.0 0.1 cholesky.224
  221.2 0.3 constant_dynamic-update-slice_fusion.2
  221.5 0.3 convolution_subtract_fusion.3
  221.8 11.7 %cholesky.217 = f32[128,128]{1,0:T(8,128)S(1)} custom-call(f32[128,128]{1,0:T(8,128)S(1)} %cholesky.270), custom_call_target="Cholesky" | custom-call | tf_op jit(solution)/shard_map/jit(cholesky)/cholesky | solution.py:20
  233.6 10.2 %custom-call.31 = f32[1,128,128]{1,2,0:T(8,128)S(1)} custom-call(f32[1,128,128]{2,1,0:T(8,128)S(1)} %get-tuple-element.26), custom_call_target="InvertDiagBlocksLowerTriangular" | custom-call | tf_op jit(solution)/shard_map/jit(cholesky)/cholesky | solution.py:20
  243.8 0.3 convolution_dynamic-update-slice_fusion
  244.0 0.4 convolution_subtract_fusion.4
  244.4 11.7 %cholesky.238 = f32[128,128]{1,0:T(8,128)S(1)} custom-call(f32[128,128]{1,0:T(8,128)S(1)} %cholesky.275), custom_call_target="Cholesky" | custom-call | tf_op jit(solution)/shard_map/jit(cholesky)/cholesky | solution.py:20
  256.2 0.7 compare_reduce_fusion.1
  256.8 9.8 %custom-call.32 = f32[1,128,128]{1,2,0:T(8,128)S(1)} custom-call(f32[1,128,128]{2,1,0:T(8,128)S(1)} %get-tuple-element.23), custom_call_target="InvertDiagBlocksLowerTriangular" | custom-call | tf_op jit(solution)/shard_map/jit(cholesky)/cholesky | solution.py:20
  266.7 0.2 convolution_dynamic-update-slice_fusion.1
  266.9 0.4 convolution_subtract_fusion.5
  267.3 11.7 %cholesky.255 = f32[128,128]{1,0:T(8,128)S(1)} custom-call(f32[128,128]{1,0:T(8,128)S(1)} %convolution_subtract_fusion.5), custom_call_target="Cholesky" | custom-call | tf_op jit(solution)/shard_map/jit(cholesky)/cholesky | solution.py:20
  279.0 0.7 compare_reduce_fusion
  279.7 0.9 compare_reduce_fusion.2
  283.1 0.1 select_select_fusion
  283.3 10.3 %while.1 = (s32[]{:T(128)}, f32[512,512]{1,0:T(8,128)S(1)}, s32[4,2]{0,1:T(2,128)S(1)}, f32[4,128,128]{2,1,0:T(8,128)}, s32[]{:T(128)}) while((s32[]{:T(128)}, f32[512,512]{1,0:T(8,128)S(1)}, s32[4,2]{0,1:T(2,128)S(1)}, f32[4,128,128]{2,1,0:T(8,128)}, s32[]{:T(128)}) %tuple.31), condition=%wide.while_cond, body=%wide.while_body.sunk | while | flops 2 | bytes 132705 | solution.py:22
  283.3 0.1 constant_dynamic-slice_fusion.2
  283.3 0.5 fusion.56
  283.9 2.0 bitcast_dynamic-update-slice_fusion.2
  285.9 0.1 constant_dynamic-slice_fusion.2
  285.9 0.5 fusion.56
  286.4 2.0 bitcast_dynamic-update-slice_fusion.2
  288.4 0.1 constant_dynamic-slice_fusion.2
  288.5 0.5 fusion.56
  289.0 2.0 bitcast_dynamic-update-slice_fusion.2
  291.0 0.1 constant_dynamic-slice_fusion.2
  291.1 0.5 fusion.56
  291.6 2.0 bitcast_dynamic-update-slice_fusion.2
  293.6 40.1 %custom-call.33 = f32[4,128,128]{1,2,0:T(8,128)S(1)} custom-call(f32[4,128,128]{2,1,0:T(8,128)} %get-tuple-element.9), custom_call_target="InvertDiagBlocksLowerTriangular" | custom-call | tf_op jit(solution)/shard_map/triangular_solve | solution.py:22
  333.7 1.2 fusion.20
  334.9 0.4 convolution_subtract_fusion.1
  335.3 0.4 fusion.32
  335.7 0.4 convolution_subtract_fusion
  336.2 0.4 fusion.30
  336.6 0.6 convolution_subtract_fusion.2
  337.3 0.4 fusion.29
  337.7 14.6 %convolution_multiply_fusion = f32[2048,512]{1,0:T(8,128)S(1)} fusion(f32[512,2048]{1,0:T(8,128)S(1)} %copy-done.1, f32[128,512]{1,0:T(8,128)S(1)} %fusion.29, f32[128,512]{1,0:T(8,128)S(1)} %fusion.30, f32[128,512]{1,0:T(8,128)S(1)} %fusion.32, f32[128,512]{1,0:T(8,128)S(1)} %fusion.20), kind=kOutput, calls=%fused_computation.3 | convolution fusion | flops 6444285952 | bytes 9437184 | tf_op jit(solution)/shard_map/dot_general | solution.py:23
  352.3 1.9 copy-done.2
  354.2 6.1 %fusion = f32[512,2048]{1,0:T(8,128)} fusion(bf16[2048,2048]{1,0:T(8,128)(2,1)S(1)} %bitcast.58, f32[2048,512]{1,0:T(8,128)S(1)} %convolution_multiply_fusion), kind=kOutput, calls=%fused_computation.4 | convolution fusion | flops 4296015872 | bytes 16777216 | tf_op jit(solution)/shard_map/dot_general | solution.py:33
  360.3 0.0 reduce-scatter.2.cloned.1.call-update
  361.0 3.1 dynamic-slice_select_fusion
  364.1 90.6 %reduce-scatter.2.cloned.1.call-done = f32[32,2048]{1,0:T(8,128)} async-done(((f32[512,2048]{1,0:T(8,128)}), f32[32,2048]{1,0:T(8,128)}) %reduce-scatter.2.cloned.1.call-update) | async-done | bytes 262160 | tf_op jit(solution)/shard_map/reduce_scatter | solution.py:32
  454.7 1.7 multiply_select_fusion
  (21 shorter events, 0.2 us)
Async XLA Ops:
  7.2 20.7 %all-gather.3.cloned.1.call-start = ((), (), s32[]{:S(2)}) async-start(), calls=%async_computation.1 | async-start | bytes 6291456 | tf_op jit(solution)/shard_map/all_gather | solution.py:15
  11.3 49.4 %all-gather.5.cloned.1.call-start = ((), (), s32[]{:S(2)}) async-start(), calls=%async_computation.2 | async-start | bytes 25165824 | tf_op jit(solution)/shard_map/all_gather | solution.py:14
  12.1 184.4 %all-reduce.3.cloned.1.call-start = ((), (), s32[]{:S(2)}) async-start(), calls=%async_computation.3 | async-start | bytes 2097152 | tf_op jit(solution)/shard_map/psum | solution.py:19
  73.7 1.9 copy-start
  83.4 371.3 %reduce-scatter.2.cloned.1.call-start = ((), (), s32[]{:S(2)}) async-start(), calls=%async_computation.4 | async-start | bytes 4456448 | tf_op jit(solution)/shard_map/reduce_scatter | solution.py:32
  333.7 4.0 copy-start.1
  336.6 17.6 %slice-start = ((s8[8388608]{0:T(1024)(128)(4,1)}), s8[4194304]{0:T(1024)(128)(4,1)S(1)}, s32[]{:S(2)}) async-start(s8[8388608]{0:T(1024)(128)(4,1)} %bitcast.57), calls=%async_computation.5 | async-start | bytes 8388608
  337.7 16.5 %slice-start.1 = ((s8[8388608]{0:T(1024)(128)(4,1)}), s8[4194304]{0:T(1024)(128)(4,1)S(1)}, s32[]{:S(2)}) async-start(s8[8388608]{0:T(1024)(128)(4,1)} %bitcast.57), calls=%async_computation.6 | async-start | bytes 8388608
  352.3 1.9 copy-start.2
Sparse Core Ops, SparseCore 0:
  11.4 16.3 all-gather.2
  29.4 31.2 all-gather.4
  83.5 112.8 all-reduce.2
  360.4 94.2 reduce-scatter.1
where the time goes:
time: 471 us; the launch traced here: 463 us
  waiting for transfers between devices  252 us (54%)
  other arithmetic  130 us (28%)
  matrix products  47.2 us (10%)
  between operations  17.5 us (4%)
  local copies, waits for them, and re-layouts  15.8 us (3%)
    psum x1, waiting for transfers between devices, on_device(): gram_matrix = lax.psum(local_gram, 'seq')  112 us
    reduce_scatter x1, waiting for transfers between devices, on_device(): lax.psum_scatter(lax.dot_general(rounded, key_rows, contract, preferred_e...  90.6 us
    another operation x14, other arithmetic, on_device(): lower_factor = jnp.linalg.cholesky(gram_matrix)  79 us
    another operation x3, other arithmetic, on_device(): lax.linalg.triangular_solve(lower_factor, identity, left_side=True, lower...  40.3 us
    all_gather x1, waiting for transfers between devices, on_device(): whole_keys = lax.all_gather(key_rows, 'grp', axis=1, tiled=True)  32.8 us
    all_gather x1, waiting for transfers between devices, on_device(): whole_probes = lax.all_gather(probes, 'grp', axis=0, tiled=True)  15.7 us
    dot_general x1, matrix products, on_device(): jnp.dot(sketch, inverse.T, precision=lax.Precision.HIGHEST) * root_tokens  14.6 us
    dot_general x1, matrix products, on_device(): jnp.dot(whole_keys, whole_probes, preferred_element_type=jnp.float32)  13 us
  transfers between devices with their start and end apart: 4, of which 4 were waited for; matrix products, arithmetic and copies ran while one was open for 1% of the time, Pallas kernels for 0%

commit v1 on v0

v1 whole, which is shorter than its diff:
```python
import functools
import math

import jax
import jax.numpy as jnp
from jax import lax
from jax.experimental import pallas as pl
from jax.experimental.pallas import tpu as pltpu
from jax.sharding import PartitionSpec as P

MESH = pl.DeviceIdType.MESH
BLOCK = 128
LAST = (((1,), (1,)), ((), ()))


def dot_f32(a, b, dims=(((1,), (0,)), ((), ()))):
    return lax.dot_general(a, b, dims, preferred_element_type=jnp.float32)


def front_kernel(
    chunk, tile, keys_hbm, ints_hbm, sketch_ref, gram_ref, basis_ref,
    keys, ints, probes, part, other, high, low, key_sem, int_sem, send_sem, recv_sem,
):
    tokens, width = keys.shape
    group = lax.axis_index("grp")
    peer = 1 - group
    chunks = tokens // chunk

    def key_copy(i):
        rows = pl.ds(pl.multiple_of(i * chunk, chunk), chunk)
        return pltpu.make_async_copy(keys_hbm.at[rows], keys.at[rows], key_sem.at[i])

    def swap(i):
        rows = pl.ds(pl.multiple_of(i * chunk, chunk), chunk)
        return pltpu.make_async_remote_copy(
            src_ref=part.at[rows], dst_ref=other.at[rows],
            send_sem=send_sem.at[i], recv_sem=recv_sem.at[i],
            device_id={"grp": peer}, device_id_type=MESH,
        )

    int_copy = pltpu.make_async_copy(ints_hbm, ints, int_sem)
    int_copy.start()
    for i in range(chunks):
        key_copy(i).start()
    barrier = pltpu.get_barrier_semaphore()
    pl.semaphore_signal(barrier, inc=1, device_id={"grp": peer}, device_id_type=MESH)
    int_copy.wait()

    @pl.loop(0, width // chunk)
    def _(i):
        rows = pl.ds(pl.multiple_of(i * chunk, chunk), chunk)
        probes[rows, :] = (ints[rows, :].astype(jnp.float32) * 0.015625).astype(jnp.bfloat16)

    pl.semaphore_wait(barrier, 1)

    @pl.loop(0, chunks)
    def _(i):
        rows = pl.ds(pl.multiple_of(i * chunk, chunk), chunk)
        key_copy(i).wait()
        part[rows, :] = dot_f32(keys[rows, :], probes[...])
        swap(i).start()

    @pl.loop(0, chunks)
    def _(i):
        start = pl.multiple_of(i * chunk, chunk)
        rows = pl.ds(start, chunk)
        swap(i).wait()
        total = part[rows, :] + other[rows, :]
        sketch_ref[rows, :] = total
        flipped = total.T
        top = flipped.astype(jnp.bfloat16)
        high[:, rows] = top
        low[:, rows] = (flipped - top.astype(jnp.float32)).astype(jnp.bfloat16)

    for t, (row0, row1, col0, col1) in enumerate(
        ((0, 1, 0, 0), (3, 1, 0, 1), (3, 2, 1, 0), (3, 2, 2, 1), (3, 2, 3, 2))
    ):
        row = pl.multiple_of((row0 + group * (row1 - row0)) * BLOCK, BLOCK)
        col = pl.multiple_of((col0 + group * (col1 - col0)) * BLOCK, BLOCK)
        row_high, row_low = high[pl.ds(row, BLOCK), :], low[pl.ds(row, BLOCK), :]
        col_high, col_low = high[pl.ds(col, BLOCK), :], low[pl.ds(col, BLOCK), :]
        gram_ref[t] = dot_f32(row_high, col_high, LAST) + (
            dot_f32(row_high, col_low, LAST) + dot_f32(row_low, col_high, LAST)
        )

    @pl.loop(0, width // tile)
    def _(j):
        cols = pl.ds(pl.multiple_of(j * tile, tile), tile)
        product = dot_f32(high[...], keys[:, cols]) + dot_f32(low[...], keys[:, cols])
        basis_ref[cols, :] = product.T


def front(key_rows, probe_ints):
    tokens, width = key_rows.shape
    count = probe_ints.shape[1]
    chunk = 256
    chunks = tokens // chunk
    vmem = pl.BlockSpec(memory_space=pltpu.VMEM)
    anyspace = pl.BlockSpec(memory_space=pl.ANY)
    return pl.pallas_call(
        functools.partial(front_kernel, chunk, 256),
        out_shape=(
            jax.ShapeDtypeStruct((tokens, count), jnp.float32),
            jax.ShapeDtypeStruct((5, BLOCK, BLOCK), jnp.float32),
            jax.ShapeDtypeStruct((width, count), jnp.float32),
        ),
        in_specs=[anyspace, anyspace],
        out_specs=(vmem, vmem, vmem),
        scratch_shapes=[
            pltpu.VMEM((tokens, width), jnp.bfloat16),
            pltpu.VMEM((width, count), jnp.int32),
            pltpu.VMEM((width, count), jnp.bfloat16),
            pltpu.VMEM((tokens, count), jnp.float32),
            pltpu.VMEM((tokens, count), jnp.float32),
            pltpu.VMEM((count, tokens), jnp.bfloat16),
            pltpu.VMEM((count, tokens), jnp.bfloat16),
            pltpu.SemaphoreType.DMA((chunks,)),
            pltpu.SemaphoreType.DMA,
            pltpu.SemaphoreType.DMA((chunks,)),
            pltpu.SemaphoreType.DMA((chunks,)),
        ],
        compiler_params=pltpu.CompilerParams(
            collective_id=0, has_side_effects=True, vmem_limit_bytes=50 << 20
        ),
        name="front",
    )(key_rows, probe_ints)


def gram_kernel(n, x_ref, out_ref, inbox, send1, recv1, send2, recv2, send3, recv3):
    me = lax.axis_index("seq")
    group = lax.axis_index("grp")
    peer = 1 - group
    barrier = pltpu.get_barrier_semaphore()

    @pl.loop(1, n)
    def _(k):
        pl.semaphore_signal(
            barrier, inc=1, device_id={"seq": lax.rem(me + k, n)}, device_id_type=MESH
        )

    pl.semaphore_signal(barrier, inc=1, device_id={"grp": peer}, device_id_type=MESH)
    pl.semaphore_wait(barrier, n)

    def scatter(k):
        to = lax.rem(me + k, n)
        return pltpu.make_async_remote_copy(
            src_ref=x_ref.at[to], dst_ref=inbox.at[k],
            send_sem=send1.at[k], recv_sem=recv1.at[k],
            device_id={"seq": to}, device_id_type=MESH,
        )

    def gather(k):
        return pltpu.make_async_remote_copy(
            src_ref=out_ref.at[group, me], dst_ref=out_ref.at[group, me],
            send_sem=send2.at[k], recv_sem=recv2.at[k],
            device_id={"seq": lax.rem(me + k, n)}, device_id_type=MESH,
        )

    def hand_over(k):
        source = lax.rem(me + n - k, n)
        return pltpu.make_async_remote_copy(
            src_ref=out_ref.at[group, source], dst_ref=out_ref.at[group, source],
            send_sem=send3.at[k], recv_sem=recv3.at[k],
            device_id={"grp": peer}, device_id_type=MESH,
        )

    @pl.loop(1, n)
    def _(k):
        scatter(k).start()

    out_ref[group, me] = x_ref[me]

    @pl.loop(1, n)
    def _(k):
        scatter(k).wait_recv()
        out_ref[group, me] += inbox[k]

    @pl.loop(1, n)
    def _(k):
        gather(k).start()

    hand_over(0).start()

    @pl.loop(1, n)
    def _(k):
        gather(k).wait_recv()
        hand_over(k).start()

    @pl.loop(1, n)
    def _(k):
        scatter(k).wait_send()
        gather(k).wait_send()
        hand_over(k).wait()

    hand_over(0).wait()


def sum_gram(blocks, n):
    size = blocks.size // BLOCK
    part = size // n
    vmem = pl.BlockSpec(memory_space=pltpu.VMEM)
    whole = pl.pallas_call(
        functools.partial(gram_kernel, n),
        out_shape=jax.ShapeDtypeStruct((2, n, part, BLOCK), jnp.float32),
        in_specs=[vmem],
        out_specs=vmem,
        scratch_shapes=[pltpu.VMEM((n, part, BLOCK), jnp.float32)]
        + [pltpu.SemaphoreType.DMA((n,))] * 6,
        compiler_params=pltpu.CompilerParams(collective_id=1, has_side_effects=True),
        name="gram_sum",
    )(blocks.reshape(n, part, BLOCK))
    return whole.reshape(2, 5, BLOCK, BLOCK)


def factor_block(a):
    panels = a.shape[0] // 8
    shape = (8, a.shape[1])
    spread = lambda v: jnp.broadcast_to(v, shape)
    sub = lax.broadcasted_iota(jnp.int32, shape, 0)
    lane = lax.broadcasted_iota(jnp.int32, shape, 1)
    rows = [a[8 * p : 8 * p + 8, :] for p in range(panels)]
    unit = [jnp.where(lane == sub + 8 * p, 1.0, 0.0).astype(jnp.float32) for p in range(panels)]
    result = []
    for p in range(panels):
        left, right = rows[p], unit[p]
        column = [spread(left[:, 8 * p + m : 8 * p + m + 1]) for m in range(8)]
        inverse_pivot = jnp.zeros(shape, jnp.float32)
        pivots = jnp.ones(shape, jnp.float32)
        for j in range(8):
            pivot = spread(column[j][j : j + 1, :])
            reciprocal = 1.0 / pivot
            factor = jnp.where(sub > j, column[j] * reciprocal, 0.0)
            for m in range(j + 1, 8):
                column[m] = column[m] - factor * spread(column[m][j : j + 1, :])
            left = left - factor * spread(left[j : j + 1, :])
            right = right - factor * spread(right[j : j + 1, :])
            inverse_pivot = jnp.where(sub == j, reciprocal, inverse_pivot)
            pivots = jnp.where(sub == j, pivot, pivots)
        result.append(right * lax.rsqrt(pivots))
        if p == panels - 1:
            break
        left, right = left * inverse_pivot, right * inverse_pivot
        for j in range(7, 0, -1):
            factor = jnp.where(sub < j, column[j] * inverse_pivot, 0.0)
            left = left - factor * spread(left[j : j + 1, :])
            right = right - factor * spread(right[j : j + 1, :])
        lefts = [spread(left[j : j + 1, :]) for j in range(8)]
        rights = [spread(right[j : j + 1, :]) for j in range(8)]
        for i in range(p + 1, panels):
            row, other = rows[i], unit[i]
            for j in range(8):
                factor = spread(rows[i][:, 8 * p + j : 8 * p + j + 1])
                row = row - factor * lefts[j]
                other = other - factor * rights[j]
            rows[i], unit[i] = row, other
    return jnp.concatenate(result, axis=0)


def exact(a, b, dims=(((1,), (0,)), ((), ()))):
    return lax.dot_general(
        a, b, dims, precision=lax.Precision.HIGHEST, preferred_element_type=jnp.float32
    )


def inverse_kernel(gram_ref, out_ref, cols):
    size = out_ref.shape[0]
    blocks = size // BLOCK
    cols[...] = jnp.zeros_like(cols)
    places = (((0, 0), (3, 0), (3, 1), (3, 2), (3, 3)), ((1, 0), (1, 1), (2, 0), (2, 1), (2, 2)))
    for group in range(2):
        for t, (i, j) in enumerate(places[group]):
            cols[j, i * BLOCK : (i + 1) * BLOCK, :] = gram_ref[group, t]
    row = lax.broadcasted_iota(jnp.int32, (size, size), 0)
    col = lax.broadcasted_iota(jnp.int32, (size, size), 1)
    out_ref[...] = jnp.where(row == col, 1.0, 0.0).astype(jnp.float32)

    @pl.loop(0, blocks)
    def _(b):
        start = pl.multiple_of(b * BLOCK, BLOCK)
        own = pl.ds(start, BLOCK)
        small = factor_block(cols[b, own, :])
        done = exact(small, out_ref[own, :])
        out_ref[own, :] = done
        below = exact(cols[b], small, LAST)
        below = jnp.where(
            lax.broadcasted_iota(jnp.int32, (size, BLOCK), 0) >= start + BLOCK, below, 0.0
        )
        cols[b] = below
        out_ref[...] -= exact(below, done)
        for j in range(1, blocks):
            cols[j] = cols[j] - jnp.where(
                j > b, exact(below, cols[b, j * BLOCK : (j + 1) * BLOCK, :], LAST), 0.0
            )


def inverse_factor(gram, size):
    vmem = pl.BlockSpec(memory_space=pltpu.VMEM)
    return pl.pallas_call(
        inverse_kernel,
        out_shape=jax.ShapeDtypeStruct((size, size), jnp.float32),
        in_specs=[vmem],
        out_specs=vmem,
        scratch_shapes=[pltpu.VMEM((size // BLOCK, size, BLOCK), jnp.float32)],
        compiler_params=pltpu.CompilerParams(vmem_limit_bytes=24 << 20),
        cost_estimate=pl.CostEstimate(
            flops=40_000_000_000, bytes_accessed=3 << 20, transcendentals=0
        ),
        name="inverse_factor",
    )(gram)


def on_device(key_rows, probe_ints, rank_keep):
    seq_count = lax.axis_size("seq")
    tokens = key_rows.shape[0] * seq_count
    root_tokens = math.sqrt(tokens)
    sketch, gram_blocks, product = front(key_rows, probe_ints)
    mixed = lax.psum_scatter(product, "seq", scatter_dimension=0, tiled=True)
    gram = sum_gram(gram_blocks, seq_count)
    probe_count = sketch.shape[1]
    inverse = inverse_factor(gram, probe_count)
    part_width = probe_count // lax.axis_size("grp")
    first_column = lax.axis_index("grp") * part_width
    columns = first_column + jnp.arange(part_width)
    own_rows = lax.dynamic_slice_in_dim(inverse, first_column, part_width, 0)
    own_columns = lax.dot_general(sketch, own_rows, LAST, precision=lax.Precision.HIGH)
    latents = jnp.where(columns[None, :] < rank_keep[0], own_columns * root_tokens, jnp.float32(0.0))
    some_columns = lax.dot_general(inverse, mixed, LAST, precision=lax.Precision.HIGH)
    row_index = jnp.arange(probe_count)
    some_columns = jnp.where(row_index[:, None] < rank_keep[0], some_columns, jnp.float32(0.0))
    latent_basis = lax.all_to_all(some_columns, "seq", split_axis=0, concat_axis=1, tiled=True)
    return (latents, latent_basis)


def solution(mesh):
    in_specs = (P("seq", "grp"), P("grp", None), P())
    out_specs = (P("seq", "grp"), P("seq", "grp"))
    return jax.shard_map(
        on_device, mesh=mesh, in_specs=in_specs, out_specs=out_specs, check_vma=False
    )
```

time: 471 us -> 163 us (0.35); the launches traced: 463 us -> 163 us
  waiting for transfers between devices: 252 us -> 38.7 us
  other arithmetic: 130 us -> 0.02 us
  Pallas kernels: 0 us -> 94 us
  matrix products: 47.2 us -> 7.59 us
  local copies, waits for them, and re-layouts: 15.8 us -> 2.53 us
  starting transfers between devices: 0.34 us -> 5.33 us
    another operation x17 -> x0, other arithmetic: 119 us -> none  [the longest x14 79 us: on_device(): lower_factor = jnp.linalg.cholesky(gram_matrix)]
    psum x1 -> x0, waiting for transfers between devices: 112 us -> none  [on_device(): gram_matrix = lax.psum(local_gram, 'seq')]
    pallas_call x0 -> x3, Pallas kernels: none -> 94 us  [the longest x1 36.4 us: inverse_factor(): pl.pallas_call(inverse_kernel, out_shape=jax.ShapeDtypeStruct((size, size...]
    reduce_scatter x1, waiting for transfers between devices: 90.6 us -> 34.1 us  [on_device(): mixed = lax.psum_scatter(product, 'seq', scatter_dimension=0, tiled=True)]
    all_gather x2 -> x0, waiting for transfers between devices: 48.6 us -> none  [the longest x1 32.8 us: on_device(): whole_keys = lax.all_gather(key_rows, 'grp', axis=1, tiled=True)]
    dot_general x4 -> x2, matrix products: 41.4 us -> 7.59 us  [the longest x1 5.36 us: on_device(): lax.dot_general(sketch, own_rows, LAST, precision=lax.Precision.HIGH)]
    another operation x17 -> x0, local copies, waits for them, and re-layouts: 10.4 us -> none
    another operation x13 -> x0, matrix products: 5.8 us -> none  [the longest x7 3.92 us: on_device(): lax.linalg.triangular_solve(lower_factor, identity, left_side=True, lower...]
  transfers between devices with their start and end apart: 4 -> 2, of which waited for: 4 -> 2; matrix products, arithmetic and copies ran while one was open for 1% -> 3% of each run, Pallas kernels for 0% -> 41%
where the time goes in v1:
time: 163 us
  Pallas kernels  94 us (58%)
  waiting for transfers between devices  38.7 us (24%)
  between operations  14.7 us (9%)
  matrix products  7.59 us (5%)
  starting transfers between devices  5.33 us (3%)
  local copies, waits for them, and re-layouts  2.53 us (2%)
    pallas_call x1, Pallas kernels, inverse_factor(): pl.pallas_call(inverse_kernel, out_shape=jax.ShapeDtypeStruct((size, size...  36.4 us
    reduce_scatter x1, waiting for transfers between devices, on_device(): mixed = lax.psum_scatter(product, 'seq', scatter_dimension=0, tiled=True)  34.1 us
    pallas_call x1, Pallas kernels, sum_gram(): pl.pallas_call(functools.partial(gram_kernel, n), out_shape=jax.ShapeDtyp...  29.8 us
    pallas_call x1, Pallas kernels, front(): pl.pallas_call(functools.partial(front_kernel, chunk, 256), out_shape=(ja...  27.8 us
    dot_general x1, matrix products, on_device(): lax.dot_general(sketch, own_rows, LAST, precision=lax.Precision.HIGH)  5.36 us
    all_to_all x1, starting transfers between devices, on_device(): lax.all_to_all(some_columns, 'seq', split_axis=0, concat_axis=1, tiled=True)  5.29 us
    all_to_all x1, waiting for transfers between devices, on_device(): lax.all_to_all(some_columns, 'seq', split_axis=0, concat_axis=1, tiled=True)  4.52 us
  transfers between devices with their start and end apart: 2, of which 2 were waited for; matrix products, arithmetic and copies ran while one was open for 3% of the time, Pallas kernels for 41%

profile of v1, /device:TPU:0, one launch (start us, length us, event | category | flops | bytes accessed | tf_op | source)
XLA Modules:
  0.0 162.9 jit_solution(14619109172059604837)
XLA Ops:
  7.2 0.0 reduce-scatter.2.cloned.1.call-start
  7.2 27.8 %front.1 = (f32[2048,512]{1,0:T(8,128)}, f32[5,128,128]{2,1,0:T(8,128)S(1)}, f32[2048,512]{1,0:T(8,128)}) custom-call(bf16[2048,2048]{1,0:T(8,128)(2,1)} %keys_hbm.1, s32[2048,512]{1,0:T(8,128)} %ints_hbm.1), custom_call_target="tpu_custom_call" | custom-call | tf_op jit(solution)/shard_map/front/pallas_call | solution.py:100
  35.0 0.0 copy-start.1
  35.0 0.7 copy-done.1
  35.7 0.0 reduce-scatter.2.cloned.1.call-update
  36.4 29.8 %gram_sum.1 = f32[2,16,40,128]{3,2,1,0:T(8,128)} custom-call(f32[16,40,128]{2,1,0:T(8,128)} %bitcast.16), custom_call_target="tpu_custom_call" | custom-call | tf_op jit(solution)/shard_map/gram_sum/pallas_call | solution.py:202
  66.2 0.0 copy-start
  66.2 1.1 copy-done
  67.3 36.4 %inverse_factor.1 = f32[512,512]{1,0:T(8,128)S(1)} custom-call(f32[2,5,128,128]{3,2,1,0:T(8,128)S(1)} %bitcast.15), custom_call_target="tpu_custom_call" | custom-call | flops 40000000000 | bytes 3145728 | tf_op jit(solution)/shard_map/inverse_factor/pallas_call | solution.py:298
  103.7 34.1 %reduce-scatter.2.cloned.1.call-done = f32[128,512]{1,0:T(8,128)} async-done(((f32[2048,512]{1,0:T(8,128)}), f32[128,512]{1,0:T(8,128)}) %reduce-scatter.2.cloned.1.call-update) | async-done | bytes 262160 | tf_op jit(solution)/shard_map/reduce_scatter | solution.py:317
  137.9 2.2 %convolution_select_fusion = f32[512,128]{1,0:T(8,128)} fusion(f32[512,512]{1,0:T(8,128)S(1)} %inverse_factor.1, f32[128,512]{1,0:T(8,128)} %reduce-scatter.2.cloned.1.call-done, pred[512]{0:T(512)(128)(4,1)S(1)} %iota_compare_fusion), kind=kOutput, calls=%fused_computation.2 | convolution fusion | flops 201392128 | bytes 1573376 | tf_op jit(solution)/shard_map/dot_general | solution.py:327
  140.1 5.3 %all-to-all-start = ((f32[16,32,128]{2,1,0:T(8,128)}), f32[16,32,128]{2,1,0:T(8,128)S(1)}, u32[]{:S(2)}, u32[]{:S(2)}) async-start(f32[16,32,128]{2,1,0:T(8,128)} %bitcast.3), calls=%async_computation.1 | async-start | bytes 524288 | tf_op jit(solution)/shard_map/all_to_all | solution.py:330
  145.4 5.4 %fusion = f32[2048,256]{1,0:T(8,128)} fusion(f32[2048,512]{1,0:T(8,128)} %get-tuple-element.5, pred[256]{0:T(512)(128)(4,1)S(1)} %add_compare_fusion, f32[512,512]{1,0:T(8,128)S(1)} %inverse_factor.1, s32[]{:T(128)S(6)} %select_n.11), kind=kOutput, calls=%fused_computation.1 | convolution fusion | flops 1611661312 | bytes 6816260 | tf_op jit(solution)/shard_map/dot_general | solution.py:325
  150.8 4.5 %all-to-all-done = f32[16,32,128]{2,1,0:T(8,128)S(1)} async-done(((f32[16,32,128]{2,1,0:T(8,128)}), f32[16,32,128]{2,1,0:T(8,128)S(1)}, u32[]{:S(2)}, u32[]{:S(2)}) %all-to-all-start) | async-done | bytes 262176 | tf_op jit(solution)/shard_map/all_to_all | solution.py:330
  155.3 0.7 copy_bitcast_fusion
  (2 shorter events, 0.0 us)
Async XLA Ops:
  7.2 130.7 %reduce-scatter.2.cloned.1.call-start = ((), (), s32[]{:S(2)}) async-start(), calls=%async_computation.2 | async-start | bytes 4456448 | tf_op jit(solution)/shard_map/reduce_scatter | solution.py:317
  35.0 0.7 copy-start.1
  66.2 1.1 copy-start
  140.1 15.2 %all-to-all-start = ((f32[16,32,128]{2,1,0:T(8,128)}), f32[16,32,128]{2,1,0:T(8,128)S(1)}, u32[]{:S(2)}, u32[]{:S(2)}) async-start(f32[16,32,128]{2,1,0:T(8,128)} %bitcast.3), calls=%async_computation.1 | async-start | bytes 524288 | tf_op jit(solution)/shard_map/all_to_all | solution.py:330
Sparse Core Ops, SparseCore 0:
  35.9 101.9 reduce-scatter.1

commit v2 on v1

--- a/solution.py
+++ b/solution.py
@@ -124,92 +124,6 @@
         ),
         name="front",
     )(key_rows, probe_ints)
-
-
-def gram_kernel(n, x_ref, out_ref, inbox, send1, recv1, send2, recv2, send3, recv3):
-    me = lax.axis_index("seq")
-    group = lax.axis_index("grp")
-    peer = 1 - group
-    barrier = pltpu.get_barrier_semaphore()
-
-    @pl.loop(1, n)
-    def _(k):
-        pl.semaphore_signal(
-            barrier, inc=1, device_id={"seq": lax.rem(me + k, n)}, device_id_type=MESH
-        )
-
-    pl.semaphore_signal(barrier, inc=1, device_id={"grp": peer}, device_id_type=MESH)
-    pl.semaphore_wait(barrier, n)
-
-    def scatter(k):
-        to = lax.rem(me + k, n)
-        return pltpu.make_async_remote_copy(
-            src_ref=x_ref.at[to], dst_ref=inbox.at[k],
-            send_sem=send1.at[k], recv_sem=recv1.at[k],
-            device_id={"seq": to}, device_id_type=MESH,
-        )
-
-    def gather(k):
-        return pltpu.make_async_remote_copy(
-            src_ref=out_ref.at[group, me], dst_ref=out_ref.at[group, me],
-            send_sem=send2.at[k], recv_sem=recv2.at[k],
-            device_id={"seq": lax.rem(me + k, n)}, device_id_type=MESH,
-        )
-
-    def hand_over(k):
-        source = lax.rem(me + n - k, n)
-        return pltpu.make_async_remote_copy(
-            src_ref=out_ref.at[group, source], dst_ref=out_ref.at[group, source],
-            send_sem=send3.at[k], recv_sem=recv3.at[k],
-            device_id={"grp": peer}, device_id_type=MESH,
-        )
-
-    @pl.loop(1, n)
-    def _(k):
-        scatter(k).start()
-
-    out_ref[group, me] = x_ref[me]
-
-    @pl.loop(1, n)
-    def _(k):
-        scatter(k).wait_recv()
-        out_ref[group, me] += inbox[k]
-
-    @pl.loop(1, n)
-    def _(k):
-        gather(k).start()
-
-    hand_over(0).start()
-
-    @pl.loop(1, n)
-    def _(k):
-        gather(k).wait_recv()
-        hand_over(k).start()
-
-    @pl.loop(1, n)
-    def _(k):
-        scatter(k).wait_send()
-        gather(k).wait_send()
-        hand_over(k).wait()
-
-    hand_over(0).wait()
-
-
-def sum_gram(blocks, n):
-    size = blocks.size // BLOCK
-    part = size // n
-    vmem = pl.BlockSpec(memory_space=pltpu.VMEM)
-    whole = pl.pallas_call(
-        functools.partial(gram_kernel, n),
-        out_shape=jax.ShapeDtypeStruct((2, n, part, BLOCK), jnp.float32),
-        in_specs=[vmem],
-        out_specs=vmem,
-        scratch_shapes=[pltpu.VMEM((n, part, BLOCK), jnp.float32)]
-        + [pltpu.SemaphoreType.DMA((n,))] * 6,
-        compiler_params=pltpu.CompilerParams(collective_id=1, has_side_effects=True),
-        name="gram_sum",
-    )(blocks.reshape(n, part, BLOCK))
-    return whole.reshape(2, 5, BLOCK, BLOCK)
 
 
 def factor_block(a):
@@ -262,20 +176,129 @@
     )
 
 
-def inverse_kernel(gram_ref, out_ref, cols):
+def middle_kernel(
+    n, inner, x_ref, product, out_ref, mixed_ref, whole, inbox, cols, near, total, far,
+    send1, recv1, send2, recv2, send3, recv3, near_send, near_recv, far_send, far_recv,
+):
+    me = lax.axis_index("seq")
+    group = lax.axis_index("grp")
+    peer = 1 - group
+    outer = n // inner
+    high, low = me // inner, lax.rem(me, inner)
+    barrier = pltpu.get_barrier_semaphore()
+
+    @pl.loop(1, n)
+    def _(k):
+        pl.semaphore_signal(
+            barrier, inc=1, device_id={"seq": lax.rem(me + k, n)}, device_id_type=MESH
+        )
+
+    pl.semaphore_signal(barrier, inc=1, device_id={"grp": peer}, device_id_type=MESH)
+    pl.semaphore_wait(barrier, n)
+
+    def scatter(k):
+        to = lax.rem(me + k, n)
+        return pltpu.make_async_remote_copy(
+            src_ref=x_ref.at[to], dst_ref=inbox.at[k],
+            send_sem=send1.at[k], recv_sem=recv1.at[k],
+            device_id={"seq": to}, device_id_type=MESH,
+        )
+
+    def gather(k):
+        return pltpu.make_async_remote_copy(
+            src_ref=whole.at[group, me], dst_ref=whole.at[group, me],
+            send_sem=send2.at[k], recv_sem=recv2.at[k],
+            device_id={"seq": lax.rem(me + k, n)}, device_id_type=MESH,
+        )
+
+    def hand_over(k):
+        source = lax.rem(me + n - k, n)
+        return pltpu.make_async_remote_copy(
+            src_ref=whole.at[group, source], dst_ref=whole.at[group, source],
+            send_sem=send3.at[k], recv_sem=recv3.at[k],
+            device_id={"grp": peer}, device_id_type=MESH,
+        )
+
+    def send_near(k):
+        to = lax.rem(low + k, inner)
+        return pltpu.make_async_remote_copy(
+            src_ref=product.at[:, to], dst_ref=near.at[k],
+            send_sem=near_send.at[k], recv_sem=near_recv.at[k],
+            device_id={"seq": high * inner + to}, device_id_type=MESH,
+        )
+
+    def send_far(k):
+        to = lax.rem(high + k, outer)
+        return pltpu.make_async_remote_copy(
+            src_ref=total.at[to], dst_ref=far.at[k],
+            send_sem=far_send.at[k], recv_sem=far_recv.at[k],
+            device_id={"seq": to * inner + low}, device_id_type=MESH,
+        )
+
+    @pl.loop(1, n)
+    def _(k):
+        scatter(k).start()
+
+    for k in range(1, inner):
+        send_near(k).start()
+
+    whole[group, me] = x_ref[me]
+
+    @pl.loop(1, n)
+    def _(k):
+        scatter(k).wait_recv()
+        whole[group, me] += inbox[k]
+
+    @pl.loop(1, n)
+    def _(k):
+        gather(k).start()
+
+    hand_over(0).start()
+
+    @pl.loop(1, n)
+    def _(k):
+        gather(k).wait_recv()
+        hand_over(k).start()
+
+    @pl.loop(1, n)
+    def _(k):
+        scatter(k).wait_send()
+        gather(k).wait_send()
+        hand_over(k).wait()
+
+    hand_over(0).wait()
+
     size = out_ref.shape[0]
     blocks = size // BLOCK
+    part = x_ref.shape[1]
     cols[...] = jnp.zeros_like(cols)
     places = (((0, 0), (3, 0), (3, 1), (3, 2), (3, 3)), ((1, 0), (1, 1), (2, 0), (2, 1), (2, 2)))
-    for group in range(2):
-        for t, (i, j) in enumerate(places[group]):
-            cols[j, i * BLOCK : (i + 1) * BLOCK, :] = gram_ref[group, t]
+    for side in range(2):
+        flat = whole[side].reshape(n * part, BLOCK)
+        for t, (i, j) in enumerate(places[side]):
+            cols[j, i * BLOCK : (i + 1) * BLOCK, :] = flat[t * BLOCK : (t + 1) * BLOCK]
     row = lax.broadcasted_iota(jnp.int32, (size, size), 0)
     col = lax.broadcasted_iota(jnp.int32, (size, size), 1)
     out_ref[...] = jnp.where(row == col, 1.0, 0.0).astype(jnp.float32)
 
     @pl.loop(0, blocks)
     def _(b):
+        @pl.when(b == blocks // 2)
+        def _():
+            for k in range(1, inner):
+                send_near(k).wait()
+
+            @pl.loop(0, outer)
+            def _(h):
+                value = product[h, low]
+                for k in range(1, inner):
+                    value = value + near[k, h]
+                total[h] = value
+
+            @pl.loop(1, outer)
+            def _(k):
+                send_far(k).start()
+
         start = pl.multiple_of(b * BLOCK, BLOCK)
         own = pl.ds(start, BLOCK)
         small = factor_block(cols[b, own, :])
@@ -292,21 +315,46 @@
                 j > b, exact(below, cols[b, j * BLOCK : (j + 1) * BLOCK, :], LAST), 0.0
             )
 
-
-def inverse_factor(gram, size):
+    mixed_ref[...] = total[high]
+
+    @pl.loop(1, outer)
+    def _(k):
+        send_far(k).wait()
+        mixed_ref[...] += far[k]
+
+
+def middle(blocks, product, n):
+    part = blocks.size // BLOCK // n
+    width, size = product.shape
+    rows = width // n
+    inner = math.gcd(n, 4)
+    outer = n // inner
     vmem = pl.BlockSpec(memory_space=pltpu.VMEM)
+    sem = pltpu.SemaphoreType.DMA
     return pl.pallas_call(
-        inverse_kernel,
-        out_shape=jax.ShapeDtypeStruct((size, size), jnp.float32),
-        in_specs=[vmem],
-        out_specs=vmem,
-        scratch_shapes=[pltpu.VMEM((size // BLOCK, size, BLOCK), jnp.float32)],
-        compiler_params=pltpu.CompilerParams(vmem_limit_bytes=24 << 20),
-        cost_estimate=pl.CostEstimate(
-            flops=40_000_000_000, bytes_accessed=3 << 20, transcendentals=0
+        functools.partial(middle_kernel, n, inner),
+        out_shape=(
+            jax.ShapeDtypeStruct((size, size), jnp.float32),
+            jax.ShapeDtypeStruct((rows, size), jnp.float32),
         ),
-        name="inverse_factor",
-    )(gram)
+        in_specs=[vmem, vmem],
+        out_specs=(vmem, vmem),
+        scratch_shapes=[
+            pltpu.VMEM((2, n, part, BLOCK), jnp.float32),
+            pltpu.VMEM((n, part, BLOCK), jnp.float32),
+            pltpu.VMEM((size // BLOCK, size, BLOCK), jnp.float32),
+            pltpu.VMEM((inner, outer, rows, size), jnp.float32),
+            pltpu.VMEM((outer, rows, size), jnp.float32),
+            pltpu.VMEM((outer, rows, size), jnp.float32),
+        ]
+        + [sem((n,))] * 6
+        + [sem((inner,))] * 2
+        + [sem((outer,))] * 2,
+        compiler_params=pltpu.CompilerParams(
+            collective_id=1, has_side_effects=True, vmem_limit_bytes=40 << 20
+        ),
+        name="middle",
+    )(blocks.reshape(n, part, BLOCK), product.reshape(outer, inner, rows, size))
 
 
 def on_device(key_rows, probe_ints, rank_keep):
@@ -314,10 +362,8 @@
     tokens = key_rows.shape[0] * seq_count
     root_tokens = math.sqrt(tokens)
     sketch, gram_blocks, product = front(key_rows, probe_ints)
-    mixed = lax.psum_scatter(product, "seq", scatter_dimension=0, tiled=True)
-    gram = sum_gram(gram_blocks, seq_count)
+    inverse, mixed = middle(gram_blocks, product, seq_count)
     probe_count = sketch.shape[1]
-    inverse = inverse_factor(gram, probe_count)
     part_width = probe_count // lax.axis_size("grp")
     first_column = lax.axis_index("grp") * part_width
     columns = first_column + jnp.arange(part_width)

time: 163 us -> 154 us (0.945)
  waiting for transfers between devices: 38.7 us -> 4.45 us
  Pallas kernels: 94 us -> 128 us
  between operations: 14.7 us -> 1.33 us
  starting transfers between devices: 5.33 us -> 10.8 us
    reduce_scatter x1 -> x0, waiting for transfers between devices: 34.1 us -> none  [on_device(): mixed = lax.psum_scatter(product, 'seq', scatter_dimension=0, tiled=True)]
    pallas_call x2 -> x1, Pallas kernels: 66.2 us -> 100 us  [middle(): pl.pallas_call(functools.partial(middle_kernel, n, inner), out_shape=(jax...]
    all_to_all x1, starting transfers between devices: 5.29 us -> 10.8 us  [on_device(): lax.all_to_all(some_columns, 'seq', split_axis=0, concat_axis=1, tiled=True)]
  transfers between devices with their start and end apart: 2 -> 1, of which waited for: 2 -> 1; matrix products, arithmetic and copies ran while one was open for 3% -> 3% of each run, Pallas kernels for 41% -> 0%
where the time goes in v2:
time: 154 us
  Pallas kernels  128 us (83%)
  starting transfers between devices  10.8 us (7%)
  matrix products  6.65 us (4%)
  waiting for transfers between devices  4.45 us (3%)
  local copies, waits for them, and re-layouts  2.9 us (2%)
    pallas_call x1, Pallas kernels, middle(): pl.pallas_call(functools.partial(middle_kernel, n, inner), out_shape=(jax...  100 us
    pallas_call x1, Pallas kernels, front(): pl.pallas_call(functools.partial(front_kernel, chunk, 256), out_shape=(ja...  27.8 us
    all_to_all x1, starting transfers between devices, on_device(): lax.all_to_all(some_columns, 'seq', split_axis=0, concat_axis=1, tiled=True)  10.8 us
    dot_general x1, matrix products, on_device(): lax.dot_general(sketch, own_rows, LAST, precision=lax.Precision.HIGH)  5.36 us
    all_to_all x1, waiting for transfers between devices, on_device(): lax.all_to_all(some_columns, 'seq', split_axis=0, concat_axis=1, tiled=True)  4.45 us
  transfers between devices with their start and end apart: 1, of which 1 were waited for; matrix products, arithmetic and copies ran while one was open for 3% of the time, Pallas kernels for 0%

profile of v2, /device:TPU:0, one launch (start us, length us, event | category | flops | bytes accessed | tf_op | source)
XLA Modules:
  0.0 153.9 jit_solution(11888221179067194362)
XLA Ops:
  1.3 27.8 %front.1 = (f32[2048,512]{1,0:T(8,128)}, f32[5,128,128]{2,1,0:T(8,128)S(1)}, f32[2048,512]{1,0:T(8,128)}) custom-call(bf16[2048,2048]{1,0:T(8,128)(2,1)} %keys_hbm.1, s32[2048,512]{1,0:T(8,128)} %ints_hbm.1), custom_call_target="tpu_custom_call" | custom-call | tf_op jit(solution)/shard_map/front/pallas_call | solution.py:100
  29.1 0.0 copy-start
  29.1 2.2 %copy-done = f32[2048,512]{1,0:T(8,128)S(1)} copy-done((f32[2048,512]{1,0:T(8,128)S(1)}, f32[2048,512]{1,0:T(8,128)}, u32[]{:S(2)}) %copy-start) | copy-done | bytes 4194328
  31.3 100.0 %middle.1 = (f32[512,512]{1,0:T(8,128)S(1)}, f32[128,512]{1,0:T(8,128)S(1)}) custom-call(f32[16,40,128]{2,1,0:T(8,128)S(1)} %bitcast.16, f32[4,4,128,512]{3,2,1,0:T(8,128)S(1)} %bitcast.15), custom_call_target="tpu_custom_call" | custom-call | tf_op jit(solution)/shard_map/middle/pallas_call | solution.py:334
  131.3 1.3 convolution_select_fusion
  132.6 10.8 %all-to-all-start = ((f32[16,32,128]{2,1,0:T(8,128)}), f32[16,32,128]{2,1,0:T(8,128)S(1)}, u32[]{:S(2)}, u32[]{:S(2)}) async-start(f32[16,32,128]{2,1,0:T(8,128)} %bitcast.3), calls=%async_computation | async-start | bytes 524288 | tf_op jit(solution)/shard_map/all_to_all | solution.py:376
  143.4 5.4 %fusion = f32[2048,256]{1,0:T(8,128)} fusion(f32[2048,512]{1,0:T(8,128)} %get-tuple-element.7, pred[256]{0:T(512)(128)(4,1)S(1)} %add_compare_fusion, f32[512,512]{1,0:T(8,128)S(1)} %get-tuple-element.10, s32[]{:T(128)S(6)} %select_n.11), kind=kOutput, calls=%fused_computation.1 | convolution fusion | flops 1611661312 | bytes 6816260 | tf_op jit(solution)/shard_map/dot_general | solution.py:371
  148.7 4.5 %all-to-all-done = f32[16,32,128]{2,1,0:T(8,128)S(1)} async-done(((f32[16,32,128]{2,1,0:T(8,128)}), f32[16,32,128]{2,1,0:T(8,128)S(1)}, u32[]{:S(2)}, u32[]{:S(2)}) %all-to-all-start) | async-done | bytes 262176 | tf_op jit(solution)/shard_map/all_to_all | solution.py:376
  153.2 0.7 copy_bitcast_fusion
  (2 shorter events, 0.0 us)
Async XLA Ops:
  29.1 2.2 %copy-start = (f32[2048,512]{1,0:T(8,128)S(1)}, f32[2048,512]{1,0:T(8,128)}, u32[]{:S(2)}) copy-start(f32[2048,512]{1,0:T(8,128)} %get-tuple-element.9) | copy-start | bytes 12582916
  132.6 20.6 %all-to-all-start = ((f32[16,32,128]{2,1,0:T(8,128)}), f32[16,32,128]{2,1,0:T(8,128)S(1)}, u32[]{:S(2)}, u32[]{:S(2)}) async-start(f32[16,32,128]{2,1,0:T(8,128)} %bitcast.3), calls=%async_computation | async-start | bytes 524288 | tf_op jit(solution)/shard_map/all_to_all | solution.py:376

commit v3 on v2

v3 whole, which is shorter than its diff:
```python
import functools
import math

import jax
import jax.numpy as jnp
from jax import lax
from jax.experimental import pallas as pl
from jax.experimental.pallas import tpu as pltpu
from jax.sharding import PartitionSpec as P

MESH = pl.DeviceIdType.MESH
BLOCK = 128
LAST = (((1,), (1,)), ((), ()))


def dot_f32(a, b, dims=(((1,), (0,)), ((), ()))):
    return lax.dot_general(a, b, dims, preferred_element_type=jnp.float32)


def factor_block(a):
    panels = a.shape[0] // 8
    shape = (8, a.shape[1])
    spread = lambda v: jnp.broadcast_to(v, shape)
    sub = lax.broadcasted_iota(jnp.int32, shape, 0)
    lane = lax.broadcasted_iota(jnp.int32, shape, 1)
    rows = [a[8 * p : 8 * p + 8, :] for p in range(panels)]
    unit = [jnp.where(lane == sub + 8 * p, 1.0, 0.0).astype(jnp.float32) for p in range(panels)]
    result = []
    for p in range(panels):
        left, right = rows[p], unit[p]
        column = [spread(left[:, 8 * p + m : 8 * p + m + 1]) for m in range(8)]
        inverse_pivot = jnp.zeros(shape, jnp.float32)
        pivots = jnp.ones(shape, jnp.float32)
        for j in range(8):
            pivot = spread(column[j][j : j + 1, :])
            reciprocal = 1.0 / pivot
            factor = jnp.where(sub > j, column[j] * reciprocal, 0.0)
            for m in range(j + 1, 8):
                column[m] = column[m] - factor * spread(column[m][j : j + 1, :])
            left = left - factor * spread(left[j : j + 1, :])
            right = right - factor * spread(right[j : j + 1, :])
            inverse_pivot = jnp.where(sub == j, reciprocal, inverse_pivot)
            pivots = jnp.where(sub == j, pivot, pivots)
        result.append(right * lax.rsqrt(pivots))
        if p == panels - 1:
            break
        left, right = left * inverse_pivot, right * inverse_pivot
        for j in range(7, 0, -1):
            factor = jnp.where(sub < j, column[j] * inverse_pivot, 0.0)
            left = left - factor * spread(left[j : j + 1, :])
            right = right - factor * spread(right[j : j + 1, :])
        lefts = [spread(left[j : j + 1, :]) for j in range(8)]
        rights = [spread(right[j : j + 1, :]) for j in range(8)]
        for i in range(p + 1, panels):
            row, other = rows[i], unit[i]
            for j in range(8):
                factor = spread(rows[i][:, 8 * p + j : 8 * p + j + 1])
                row = row - factor * lefts[j]
                other = other - factor * rights[j]
            rows[i], unit[i] = row, other
    return jnp.concatenate(result, axis=0)


def exact(a, b, dims=(((1,), (0,)), ((), ()))):
    return lax.dot_general(
        a, b, dims, precision=lax.Precision.HIGHEST, preferred_element_type=jnp.float32
    )


def whole_kernel(
    n, inner, chunk, tile, keys_hbm, ints_hbm, sketch_hbm, out_ref, mixed_ref,
    keys, ints, probes, part, other, high, low, packed, product,
    whole, inbox, cols, near, total, far,
    key_sem, int_sem, sketch_sem, send_sem, recv_sem,
    send1, recv1, send2, recv2, send3, recv3, near_send, near_recv, far_send, far_recv,
):
    tokens, width = keys.shape
    me = lax.axis_index("seq")
    group = lax.axis_index("grp")
    peer = 1 - group
    outer = n // inner
    mine, place = me // inner, lax.rem(me, inner)
    chunks = tokens // chunk
    size = out_ref.shape[0]
    blocks = size // BLOCK
    rows_each = product.shape[2]
    step = rows_each // blocks

    def key_copy(i):
        rows = pl.ds(pl.multiple_of(i * chunk, chunk), chunk)
        return pltpu.make_async_copy(keys_hbm.at[rows], keys.at[rows], key_sem.at[i])

    def swap(i):
        rows = pl.ds(pl.multiple_of(i * chunk, chunk), chunk)
        return pltpu.make_async_remote_copy(
            src_ref=part.at[rows], dst_ref=other.at[rows],
            send_sem=send_sem.at[i], recv_sem=recv_sem.at[i],
            device_id={"grp": peer}, device_id_type=MESH,
        )

    int_copy = pltpu.make_async_copy(ints_hbm, ints, int_sem)
    int_copy.start()
    for i in range(chunks):
        key_copy(i).start()
    barrier = pltpu.get_barrier_semaphore()

    @pl.loop(1, n)
    def _(k):
        pl.semaphore_signal(
            barrier, inc=1, device_id={"seq": lax.rem(me + k, n)}, device_id_type=MESH
        )

    pl.semaphore_signal(barrier, inc=1, device_id={"grp": peer}, device_id_type=MESH)
    int_copy.wait()

    @pl.loop(0, width // chunk)
    def _(i):
        rows = pl.ds(pl.multiple_of(i * chunk, chunk), chunk)
        probes[rows, :] = (ints[rows, :].astype(jnp.float32) * 0.015625).astype(jnp.bfloat16)

    pl.semaphore_wait(barrier, n)

    @pl.loop(0, chunks)
    def _(i):
        rows = pl.ds(pl.multiple_of(i * chunk, chunk), chunk)
        key_copy(i).wait()
        part[rows, :] = dot_f32(keys[rows, :], probes[...])
        swap(i).start()

    @pl.loop(0, chunks)
    def _(i):
        start = pl.multiple_of(i * chunk, chunk)
        rows = pl.ds(start, chunk)
        swap(i).wait()
        summed = part[rows, :] + other[rows, :]
        part[rows, :] = summed
        flipped = summed.T
        top = flipped.astype(jnp.bfloat16)
        high[:, rows] = top
        low[:, rows] = (flipped - top.astype(jnp.float32)).astype(jnp.bfloat16)

    def scatter(k):
        to = lax.rem(me + k, n)
        return pltpu.make_async_remote_copy(
            src_ref=packed.at[to], dst_ref=inbox.at[k],
            send_sem=send1.at[k], recv_sem=recv1.at[k],
            device_id={"seq": to}, device_id_type=MESH,
        )

    def gather(k):
        return pltpu.make_async_remote_copy(
            src_ref=whole.at[group, me], dst_ref=whole.at[group, me],
            send_sem=send2.at[k], recv_sem=recv2.at[k],
            device_id={"seq": lax.rem(me + k, n)}, device_id_type=MESH,
        )

    def hand_over(k):
        source = lax.rem(me + n - k, n)
        return pltpu.make_async_remote_copy(
            src_ref=whole.at[group, source], dst_ref=whole.at[group, source],
            send_sem=send3.at[k], recv_sem=recv3.at[k],
            device_id={"grp": peer}, device_id_type=MESH,
        )

    def piece(c):
        return pl.ds(pl.multiple_of(c * step, step), step)

    def send_near(c, k):
        to = lax.rem(place + k, inner)
        return pltpu.make_async_remote_copy(
            src_ref=product.at[:, to, piece(c)], dst_ref=near.at[k, :, piece(c)],
            send_sem=near_send.at[c, k], recv_sem=near_recv.at[c, k],
            device_id={"seq": mine * inner + to}, device_id_type=MESH,
        )

    def send_far(c, k):
        to = lax.rem(mine + k, outer)
        return pltpu.make_async_remote_copy(
            src_ref=total.at[to, piece(c)], dst_ref=far.at[k, piece(c)],
            send_sem=far_send.at[c, k], recv_sem=far_recv.at[c, k],
            device_id={"seq": to * inner + place}, device_id_type=MESH,
        )

    def pass_on(c):
        for k in range(1, inner):
            send_near(c, k).wait()

        @pl.loop(0, outer)
        def _(h):
            value = product[h, place, piece(c), :]
            for k in range(1, inner):
                value = value + near[k, h, piece(c), :]
            total[h, piece(c), :] = value

        @pl.loop(1, outer)
        def _(k):
            send_far(c, k).start()

    sketch_copy = pltpu.make_async_copy(part, sketch_hbm, sketch_sem)
    sketch_copy.start()

    found = []
    for t, (row0, row1, col0, col1) in enumerate(
        ((0, 1, 0, 0), (3, 1, 0, 1), (3, 2, 1, 0), (3, 2, 2, 1), (3, 2, 3, 2))
    ):
        row = pl.multiple_of((row0 + group * (row1 - row0)) * BLOCK, BLOCK)
        col = pl.multiple_of((col0 + group * (col1 - col0)) * BLOCK, BLOCK)
        row_high, row_low = high[pl.ds(row, BLOCK), :], low[pl.ds(row, BLOCK), :]
        col_high, col_low = high[pl.ds(col, BLOCK), :], low[pl.ds(col, BLOCK), :]
        found.append(
            dot_f32(row_high, col_high, LAST)
            + (dot_f32(row_high, col_low, LAST) + dot_f32(row_low, col_high, LAST))
        )

    packed[...] = jnp.concatenate(found, axis=0).reshape(packed.shape)

    @pl.loop(1, n)
    def _(k):
        scatter(k).start()

    @pl.loop(0, width // tile)
    def _(j):
        own = pl.ds(pl.multiple_of(j * tile, tile), tile)
        piled = (dot_f32(high[...], keys[:, own]) + dot_f32(low[...], keys[:, own])).T
        for u in range(tile // rows_each):
            q = j * (tile // rows_each) + u
            product[q // inner, lax.rem(q, inner)] = piled[u * rows_each : (u + 1) * rows_each]

    whole[group, me] = packed[me]

    @pl.loop(1, n)
    def _(k):
        scatter(k).wait_recv()
        whole[group, me] += inbox[k]

    @pl.loop(1, n)
    def _(k):
        gather(k).start()

    hand_over(0).start()

    for k in range(1, inner):
        send_near(0, k).start()

    @pl.loop(1, n)
    def _(k):
        gather(k).wait_recv()
        hand_over(k).start()

    for c in range(1, blocks):
        for k in range(1, inner):
            send_near(c, k).start()

    @pl.loop(1, n)
    def _(k):
        scatter(k).wait_send()
        gather(k).wait_send()
        hand_over(k).wait()

    hand_over(0).wait()

    cols[...] = jnp.zeros_like(cols)
    places = (((0, 0), (3, 0), (3, 1), (3, 2), (3, 3)), ((1, 0), (1, 1), (2, 0), (2, 1), (2, 2)))
    for side in range(2):
        flat = whole[side].reshape(n * packed.shape[1], BLOCK)
        for t, (i, j) in enumerate(places[side]):
            cols[j, i * BLOCK : (i + 1) * BLOCK, :] = flat[t * BLOCK : (t + 1) * BLOCK]
    row = lax.broadcasted_iota(jnp.int32, (size, size), 0)
    col = lax.broadcasted_iota(jnp.int32, (size, size), 1)
    out_ref[...] = jnp.where(row == col, 1.0, 0.0).astype(jnp.float32)

    @pl.loop(0, blocks)
    def _(b):
        @pl.when(b >= 1)
        def _():
            pass_on(b - 1)

        start = pl.multiple_of(b * BLOCK, BLOCK)
        own = pl.ds(start, BLOCK)
        small = factor_block(cols[b, own, :])
        done = exact(small, out_ref[own, :])
        out_ref[own, :] = done
        below = exact(cols[b], small, LAST)
        below = jnp.where(
            lax.broadcasted_iota(jnp.int32, (size, BLOCK), 0) >= start + BLOCK, below, 0.0
        )
        cols[b] = below
        out_ref[...] -= exact(below, done)
        for j in range(1, blocks):
            cols[j] = cols[j] - jnp.where(
                j > b, exact(below, cols[b, j * BLOCK : (j + 1) * BLOCK, :], LAST), 0.0
            )

    pass_on(blocks - 1)
    sketch_copy.wait()
    mixed_ref[...] = total[mine]

    @pl.loop(0, blocks)
    def _(c):
        @pl.loop(1, outer)
        def _(k):
            send_far(c, k).wait()
            mixed_ref[piece(c), :] += far[k, piece(c), :]


def run_whole(key_rows, probe_ints, n):
    tokens, width = key_rows.shape
    size = probe_ints.shape[1]
    chunk, tile = 256, 256
    chunks, blocks = tokens // chunk, size // BLOCK
    part = 5 * BLOCK // n
    rows = width // n
    inner = math.gcd(n, 4)
    outer = n // inner
    vmem = pl.BlockSpec(memory_space=pltpu.VMEM)
    anyspace = pl.BlockSpec(memory_space=pl.ANY)
    sem = pltpu.SemaphoreType.DMA
    return pl.pallas_call(
        functools.partial(whole_kernel, n, inner, chunk, tile),
        out_shape=(
            jax.ShapeDtypeStruct((tokens, size), jnp.float32),
            jax.ShapeDtypeStruct((size, size), jnp.float32),
            jax.ShapeDtypeStruct((rows, size), jnp.float32),
        ),
        in_specs=[anyspace, anyspace],
        out_specs=(anyspace, vmem, vmem),
        scratch_shapes=[
            pltpu.VMEM((tokens, width), jnp.bfloat16),
            pltpu.VMEM((width, size), jnp.int32),
            pltpu.VMEM((width, size), jnp.bfloat16),
            pltpu.VMEM((tokens, size), jnp.float32),
            pltpu.VMEM((tokens, size), jnp.float32),
            pltpu.VMEM((size, tokens), jnp.bfloat16),
            pltpu.VMEM((size, tokens), jnp.bfloat16),
            pltpu.VMEM((n, part, BLOCK), jnp.float32),
            pltpu.VMEM((outer, inner, rows, size), jnp.float32),
            pltpu.VMEM((2, n, part, BLOCK), jnp.float32),
            pltpu.VMEM((n, part, BLOCK), jnp.float32),
            pltpu.VMEM((blocks, size, BLOCK), jnp.float32),
            pltpu.VMEM((inner, outer, rows, size), jnp.float32),
            pltpu.VMEM((outer, rows, size), jnp.float32),
            pltpu.VMEM((outer, rows, size), jnp.float32),
            sem((chunks,)), sem, sem, sem((chunks,)), sem((chunks,)),
        ]
        + [sem((n,))] * 6
        + [sem((blocks, inner))] * 2
        + [sem((blocks, outer))] * 2,
        compiler_params=pltpu.CompilerParams(
            collective_id=0, has_side_effects=True, vmem_limit_bytes=56 << 20
        ),
        name="whole",
    )(key_rows, probe_ints)


def on_device(key_rows, probe_ints, rank_keep):
    seq_count = lax.axis_size("seq")
    tokens = key_rows.shape[0] * seq_count
    root_tokens = math.sqrt(tokens)
    sketch, inverse, mixed = run_whole(key_rows, probe_ints, seq_count)
    probe_count = sketch.shape[1]
    part_width = probe_count // lax.axis_size("grp")
    first_column = lax.axis_index("grp") * part_width
    columns = first_column + jnp.arange(part_width)
    own_rows = lax.dynamic_slice_in_dim(inverse, first_column, part_width, 0)
    own_columns = lax.dot_general(sketch, own_rows, LAST, precision=lax.Precision.HIGH)
    latents = jnp.where(columns[None, :] < rank_keep[0], own_columns * root_tokens, jnp.float32(0.0))
    some_columns = lax.dot_general(inverse, mixed, LAST, precision=lax.Precision.HIGH)
    row_index = jnp.arange(probe_count)
    some_columns = jnp.where(row_index[:, None] < rank_keep[0], some_columns, jnp.float32(0.0))
    latent_basis = lax.all_to_all(some_columns, "seq", split_axis=0, concat_axis=1, tiled=True)
    return (latents, latent_basis)


def solution(mesh):
    in_specs = (P("seq", "grp"), P("grp", None), P())
    out_specs = (P("seq", "grp"), P("seq", "grp"))
    return jax.shard_map(
        on_device, mesh=mesh, in_specs=in_specs, out_specs=out_specs, check_vma=False
    )
```

time: 154 us -> 108 us (0.70)
  Pallas kernels: 128 us -> 89.7 us
  starting transfers between devices: 10.8 us -> 4.43 us
  local copies, waits for them, and re-layouts: 2.9 us -> 0.72 us
    pallas_call x2 -> x1, Pallas kernels: 128 us -> 89.7 us  [run_whole(): pl.pallas_call(functools.partial(whole_kernel, n, inner, chunk, tile), ou...]
    all_to_all x1, starting transfers between devices: 10.8 us -> 4.43 us  [on_device(): lax.all_to_all(some_columns, 'seq', split_axis=0, concat_axis=1, tiled=True)]
    unnamed x2 -> x0, local copies, waits for them, and re-layouts: 2.18 us -> none
  transfers between devices with their start and end apart: 1 -> 1, of which waited for: 1 -> 1; matrix products, arithmetic and copies ran while one was open for 3% -> 5% of each run, Pallas kernels for 0% -> 0%
where the time goes in v3:
time: 108 us
  Pallas kernels  89.7 us (83%)
  matrix products  8.03 us (7%)
  starting transfers between devices  4.43 us (4%)
  waiting for transfers between devices  3.98 us (4%)
  between operations  1.31 us (1%)
    pallas_call x1, Pallas kernels, run_whole(): pl.pallas_call(functools.partial(whole_kernel, n, inner, chunk, tile), ou...  89.7 us
    dot_general x1, matrix products, on_device(): lax.dot_general(sketch, own_rows, LAST, precision=lax.Precision.HIGH)  5.47 us
    all_to_all x1, starting transfers between devices, on_device(): lax.all_to_all(some_columns, 'seq', split_axis=0, concat_axis=1, tiled=True)  4.43 us
    all_to_all x1, waiting for transfers between devices, on_device(): lax.all_to_all(some_columns, 'seq', split_axis=0, concat_axis=1, tiled=True)  3.98 us
    dot_general x1, matrix products, on_device(): lax.dot_general(inverse, mixed, LAST, precision=lax.Precision.HIGH)  2.55 us
  transfers between devices with their start and end apart: 1, of which 1 were waited for; matrix products, arithmetic and copies ran while one was open for 5% of the time, Pallas kernels for 0%

profile of v3, /device:TPU:0, one launch (start us, length us, event | category | flops | bytes accessed | tf_op | source)
XLA Modules:
  0.0 108.2 jit_solution(10712905956532485337)
XLA Ops:
  1.3 89.7 %whole.1 = (f32[2048,512]{1,0:T(8,128)}, f32[512,512]{1,0:T(8,128)}, f32[128,512]{1,0:T(8,128)}) custom-call(bf16[2048,2048]{1,0:T(8,128)(2,1)} %keys_hbm.1, s32[2048,512]{1,0:T(8,128)} %ints_hbm.1), custom_call_target="tpu_custom_call" | custom-call | tf_op jit(solution)/shard_map/whole/pallas_call | solution.py:318
  91.0 2.6 %convolution_select_fusion = f32[512,128]{1,0:T(8,128)} fusion(f32[512,512]{1,0:T(8,128)} %get-tuple-element.6, f32[128,512]{1,0:T(8,128)} %get-tuple-element.7, pred[512]{0:T(512)(128)(4,1)S(1)} %iota_compare_fusion), kind=kOutput, calls=%fused_computation.2 | convolution fusion | flops 201392128 | bytes 1573376 | tf_op jit(solution)/shard_map/dot_general | solution.py:367
  93.6 4.4 %all-to-all-start = ((f32[16,32,128]{2,1,0:T(8,128)}), f32[16,32,128]{2,1,0:T(8,128)S(1)}, u32[]{:S(2)}, u32[]{:S(2)}) async-start(f32[16,32,128]{2,1,0:T(8,128)} %bitcast.1), calls=%async_computation | async-start | bytes 524288 | tf_op jit(solution)/shard_map/all_to_all | solution.py:370
  98.0 5.5 %fusion = f32[2048,256]{1,0:T(8,128)} fusion(f32[2048,512]{1,0:T(8,128)} %get-tuple-element.5, pred[256]{0:T(512)(128)(4,1)S(1)} %add_compare_fusion, f32[512,512]{1,0:T(8,128)} %get-tuple-element.6, s32[]{:T(128)S(6)} %select_n.11), kind=kOutput, calls=%fused_computation.1 | convolution fusion | flops 1611661312 | bytes 6816004 | tf_op jit(solution)/shard_map/dot_general | solution.py:365
  103.5 4.0 %all-to-all-done = f32[16,32,128]{2,1,0:T(8,128)S(1)} async-done(((f32[16,32,128]{2,1,0:T(8,128)}), f32[16,32,128]{2,1,0:T(8,128)S(1)}, u32[]{:S(2)}, u32[]{:S(2)}) %all-to-all-start) | async-done | bytes 262176 | tf_op jit(solution)/shard_map/all_to_all | solution.py:370
  107.5 0.7 copy_bitcast_fusion
  (2 shorter events, 0.0 us)
Async XLA Ops:
  93.6 13.9 %all-to-all-start = ((f32[16,32,128]{2,1,0:T(8,128)}), f32[16,32,128]{2,1,0:T(8,128)S(1)}, u32[]{:S(2)}, u32[]{:S(2)}) async-start(f32[16,32,128]{2,1,0:T(8,128)} %bitcast.1), calls=%async_computation | async-start | bytes 524288 | tf_op jit(solution)/shard_map/all_to_all | solution.py:370

commit v4 on v3

--- a/solution.py
+++ b/solution.py
@@ -68,10 +68,11 @@
 
 
 def whole_kernel(
-    n, inner, chunk, tile, keys_hbm, ints_hbm, sketch_hbm, out_ref, mixed_ref,
+    n, inner, chunk, tile, root_tokens, keys_hbm, ints_hbm, latent_ref, spread_ref,
+    out_ref, mixed_ref, boxed, arrived,
     keys, ints, probes, part, other, high, low, packed, product,
     whole, inbox, cols, near, total, far,
-    key_sem, int_sem, sketch_sem, send_sem, recv_sem,
+    key_sem, int_sem, send_sem, recv_sem, send4, recv4,
     send1, recv1, send2, recv2, send3, recv3, near_send, near_recv, far_send, far_recv,
 ):
     tokens, width = keys.shape
@@ -196,9 +197,6 @@
         def _(k):
             send_far(c, k).start()
 
-    sketch_copy = pltpu.make_async_copy(part, sketch_hbm, sketch_sem)
-    sketch_copy.start()
-
     found = []
     for t, (row0, row1, col0, col1) in enumerate(
         ((0, 1, 0, 0), (3, 1, 0, 1), (3, 2, 1, 0), (3, 2, 2, 1), (3, 2, 3, 2))
@@ -292,7 +290,32 @@
             )
 
     pass_on(blocks - 1)
-    sketch_copy.wait()
+    span = latent_ref.shape[1]
+    inverse = out_ref[pl.ds(pl.multiple_of(group * span, span), span), :]
+    inverse_high = inverse.astype(jnp.bfloat16)
+    inverse_low = (inverse - inverse_high.astype(jnp.float32)).astype(jnp.bfloat16)
+
+    def latents(first, last):
+        @pl.loop(first, last)
+        def _(i):
+            rows = pl.ds(pl.multiple_of(i * chunk, chunk), chunk)
+            value = part[rows, :]
+            top = value.astype(jnp.bfloat16)
+            rest = (value - top.astype(jnp.float32)).astype(jnp.bfloat16)
+            latent_ref[rows, :] = root_tokens * (
+                dot_f32(top, inverse_high, LAST)
+                + (dot_f32(top, inverse_low, LAST) + dot_f32(rest, inverse_high, LAST))
+            )
+
+    def deal(k):
+        to = lax.rem(me + k, n)
+        return pltpu.make_async_remote_copy(
+            src_ref=boxed.at[to], dst_ref=arrived.at[me],
+            send_sem=send4.at[k], recv_sem=recv4.at[k],
+            device_id={"seq": to}, device_id_type=MESH,
+        )
+
+    latents(0, chunks // 2)
     mixed_ref[...] = total[mine]
 
     @pl.loop(0, blocks)
@@ -302,8 +325,23 @@
             send_far(c, k).wait()
             mixed_ref[piece(c), :] += far[k, piece(c), :]
 
-
-def run_whole(key_rows, probe_ints, n):
+    boxed[...] = exact(out_ref[...], mixed_ref[...], LAST).reshape(boxed.shape)
+
+    @pl.loop(1, n)
+    def _(k):
+        deal(k).start()
+
+    arrived[me] = boxed[me]
+    latents(chunks // 2, chunks)
+
+    @pl.loop(1, n)
+    def _(k):
+        deal(k).wait()
+
+    spread_ref[...] = arrived[...]
+
+
+def run_whole(key_rows, probe_ints, n, span, root_tokens):
     tokens, width = key_rows.shape
     size = probe_ints.shape[1]
     chunk, tile = 256, 256
@@ -316,15 +354,18 @@
     anyspace = pl.BlockSpec(memory_space=pl.ANY)
     sem = pltpu.SemaphoreType.DMA
     return pl.pallas_call(
-        functools.partial(whole_kernel, n, inner, chunk, tile),
+        functools.partial(whole_kernel, n, inner, chunk, tile, root_tokens),
         out_shape=(
-            jax.ShapeDtypeStruct((tokens, size), jnp.float32),
-            jax.ShapeDtypeStruct((size, size), jnp.float32),
-            jax.ShapeDtypeStruct((rows, size), jnp.float32),
+            jax.ShapeDtypeStruct((tokens, span), jnp.float32),
+            jax.ShapeDtypeStruct((n, size // n, rows), jnp.float32),
         ),
         in_specs=[anyspace, anyspace],
-        out_specs=(anyspace, vmem, vmem),
+        out_specs=(vmem, vmem),
         scratch_shapes=[
+            pltpu.VMEM((size, size), jnp.float32),
+            pltpu.VMEM((rows, size), jnp.float32),
+            pltpu.VMEM((n, size // n, rows), jnp.float32),
+            pltpu.VMEM((n, size // n, rows), jnp.float32),
             pltpu.VMEM((tokens, width), jnp.bfloat16),
             pltpu.VMEM((width, size), jnp.int32),
             pltpu.VMEM((width, size), jnp.bfloat16),
@@ -340,9 +381,9 @@
             pltpu.VMEM((inner, outer, rows, size), jnp.float32),
             pltpu.VMEM((outer, rows, size), jnp.float32),
             pltpu.VMEM((outer, rows, size), jnp.float32),
-            sem((chunks,)), sem, sem, sem((chunks,)), sem((chunks,)),
+            sem((chunks,)), sem, sem((chunks,)), sem((chunks,)),
         ]
-        + [sem((n,))] * 6
+        + [sem((n,))] * 8
         + [sem((blocks, inner))] * 2
         + [sem((blocks, outer))] * 2,
         compiler_params=pltpu.CompilerParams(
@@ -356,18 +397,15 @@
     seq_count = lax.axis_size("seq")
     tokens = key_rows.shape[0] * seq_count
     root_tokens = math.sqrt(tokens)
-    sketch, inverse, mixed = run_whole(key_rows, probe_ints, seq_count)
-    probe_count = sketch.shape[1]
+    probe_count = probe_ints.shape[1]
     part_width = probe_count // lax.axis_size("grp")
-    first_column = lax.axis_index("grp") * part_width
-    columns = first_column + jnp.arange(part_width)
-    own_rows = lax.dynamic_slice_in_dim(inverse, first_column, part_width, 0)
-    own_columns = lax.dot_general(sketch, own_rows, LAST, precision=lax.Precision.HIGH)
-    latents = jnp.where(columns[None, :] < rank_keep[0], own_columns * root_tokens, jnp.float32(0.0))
-    some_columns = lax.dot_general(inverse, mixed, LAST, precision=lax.Precision.HIGH)
-    row_index = jnp.arange(probe_count)
-    some_columns = jnp.where(row_index[:, None] < rank_keep[0], some_columns, jnp.float32(0.0))
-    latent_basis = lax.all_to_all(some_columns, "seq", split_axis=0, concat_axis=1, tiled=True)
+    own_columns, dealt = run_whole(key_rows, probe_ints, seq_count, part_width, root_tokens)
+    columns = lax.axis_index("grp") * part_width + jnp.arange(part_width)
+    latents = jnp.where(columns[None, :] < rank_keep[0], own_columns, jnp.float32(0.0))
+    rows_out = probe_count // seq_count
+    row_index = lax.axis_index("seq") * rows_out + jnp.arange(rows_out)
+    own_rows = jnp.transpose(dealt, (1, 0, 2)).reshape(rows_out, -1)
+    latent_basis = jnp.where(row_index[:, None] < rank_keep[0], own_rows, jnp.float32(0.0))
     return (latents, latent_basis)
 
 

time: 108 us -> 102 us (0.944)
  matrix products: 8.03 us -> 0 us
  Pallas kernels: 89.7 us -> 96.9 us
  starting transfers between devices: 4.43 us -> 0 us
  waiting for transfers between devices: 3.98 us -> 0 us
  other arithmetic: 0.01 us -> 3.89 us
    dot_general x2 -> x0, matrix products: 8.03 us -> none  [the longest x1 5.47 us: on_device(): lax.dot_general(sketch, own_rows, LAST, precision=lax.Precision.HIGH)]
    pallas_call x1, Pallas kernels: 89.7 us -> 96.9 us  [run_whole(): pl.pallas_call(functools.partial(whole_kernel, n, inner, chunk, tile, roo...]
    all_to_all x1 -> x0, starting transfers between devices: 4.43 us -> none  [on_device(): lax.all_to_all(some_columns, 'seq', split_axis=0, concat_axis=1, tiled=True)]
    all_to_all x1 -> x0, waiting for transfers between devices: 3.98 us -> none  [on_device(): lax.all_to_all(some_columns, 'seq', split_axis=0, concat_axis=1, tiled=True)]
    select_n x0 -> x2, other arithmetic: none -> 3.88 us  [the longest x1 3.09 us: on_device(): jnp.where(columns[None, :] < rank_keep[0], own_columns, jnp.float32(0.0))]
  transfers between devices with their start and end apart: 1 -> 0, of which waited for: 1 -> 0; matrix products, arithmetic and copies ran while one was open for 5% -> 0% of each run, Pallas kernels for 0% -> 0%
where the time goes in v4:
time: 102 us
  Pallas kernels  96.9 us (95%)
  other arithmetic  3.89 us (4%)
  between operations  1.31 us (1%)
    pallas_call x1, Pallas kernels, run_whole(): pl.pallas_call(functools.partial(whole_kernel, n, inner, chunk, tile, roo...  96.9 us
    select_n x1, other arithmetic, on_device(): jnp.where(columns[None, :] < rank_keep[0], own_columns, jnp.float32(0.0))  3.09 us

profile of v4, /device:TPU:0, one launch (start us, length us, event | category | flops | bytes accessed | tf_op | source)
XLA Modules:
  0.0 102.1 jit_solution(15086512301304994096)
XLA Ops:
  1.3 96.9 %whole.1 = (f32[2048,256]{1,0:T(8,128)}, f32[16,32,128]{2,1,0:T(8,128)}) custom-call(bf16[2048,2048]{1,0:T(8,128)(2,1)} %keys_hbm.1, s32[2048,512]{1,0:T(8,128)} %ints_hbm.1), custom_call_target="tpu_custom_call" | custom-call | tf_op jit(solution)/shard_map/whole/pallas_call | solution.py:356
  98.2 0.0 copy-start
  98.3 3.1 %broadcast_select_fusion = f32[2048,256]{1,0:T(8,128)} fusion(f32[2048,256]{1,0:T(8,128)} %get-tuple-element.4, pred[256]{0:T(512)(128)(4,1)S(1)} %add_compare_fusion), kind=kLoop, calls=%fused_computation | loop fusion | flops 524288 | bytes 4194560 | tf_op jit(solution)/shard_map/jit(_where)/select_n | solution.py:404
  101.3 0.0 copy-done
  101.3 0.8 bitcast_select_fusion
  (2 shorter events, 0.0 us)
Async XLA Ops:
  98.2 3.1 %copy-start = (f32[16,32,128]{2,1,0:T(8,128)S(1)}, f32[16,32,128]{2,1,0:T(8,128)}, u32[]{:S(2)}) copy-start(f32[16,32,128]{2,1,0:T(8,128)} %get-tuple-element.5) | copy-start | bytes 786436
